TPU v7x, 32 devices: a whole 2x2x4 slice. The times are simulated.
32 devices in a mesh: dp: 8 (over z, x), tensor: 4 (over y, core).
Axes of the slice: x: 2, y: 2, z: 4, core: 2. Of those that a mesh axis runs over, the one named last changes fastest.
Arguments:
- tokens: bfloat16 [1024, 8192], P('dp', 'tensor'), may hold values from -6 to 6
- key_value_weight: bfloat16 [8192, 2048], P('tensor'), may hold values from -0.0625 to 0.0625
- adapter_down_weight: bfloat16 [24, 64, 8192], P('dp', None, 'tensor'), may hold values from -0.0625 to 0.0625
- adapter_up_weight: bfloat16 [24, 64, 2048], P('dp', None, 'tensor'), may hold values from -0.75 to 0.75
- cotangent: bfloat16 [1024, 2048], P('dp', 'tensor'), may hold values from -3 to 3
- sequence_adapter_index: int32 [32], replicated, may hold values from 0 to 23, as said below
- adapter_storage_row: int32 [24], replicated, may hold values from 0 to 23, as said below
Outputs:
- key_value_output: bfloat16 [1024, 2048], P('dp', 'tensor')
- token_gradient: bfloat16 [1024, 8192], P('dp', 'tensor')
- grad_down: float32 [24, 64, 8192], P('dp', None, 'tensor')
- grad_up: float32 [24, 64, 2048], P('dp', None, 'tensor')
Inputs may be any that keep to these rules, and one draw needn't show every extreme that they name: Each value appears once: adapter a is held at row adapter_storage_row[a] of adapter_down_weight, adapter_up_weight, grad_down and grad_up, on index adapter_storage_row[a] // 3 of dp. `sequence_adapter_index`: the 4 sequences i that share one value of i // 4 use adapters held on 4 different indices of dp.
All inputs are finite; a program needn't handle non-finite values.
Results may differ from a plain program's by a relative error of at most 0.02.
Values may be sent and summed in bfloat16 or wider, within the bound.
A program may use at most 64 MiB of HBM per device.

v0:
```python
import jax
import jax.numpy as jnp
from jax import lax
from jax.sharding import PartitionSpec as P

adapter_scale = 0.25


def on_device(
    tokens,
    key_value_weight,
    adapter_down_weight,
    adapter_up_weight,
    cotangent,
    sequence_adapter_index,
    adapter_storage_row,
):
    dp_count = lax.axis_size("dp")
    my_index = lax.axis_index("dp")
    resident_adapters = adapter_down_weight.shape[0]
    rank_span = adapter_down_weight.shape[1]
    block_span = adapter_down_weight.shape[2]
    output_block = adapter_up_weight.shape[2]
    token_row_matrix = tokens.shape[0]
    adapters = adapter_storage_row.shape[0]
    seq_local = sequence_adapter_index.shape[0] // dp_count
    seq_length = token_row_matrix // seq_local
    adapter_codes = jnp.arange(adapters, dtype=jnp.int32)
    matches = sequence_adapter_index[:, None] == adapter_codes[None, :]
    seq_rows = jnp.sum(jnp.where(matches, adapter_storage_row[None, :], 0), axis=1)
    my_rows = lax.dynamic_slice_in_dim(seq_rows, my_index * seq_local, seq_local)
    my_owners = my_rows // resident_adapters
    owner_codes = jnp.arange(dp_count, dtype=jnp.int32)
    from_owner = (my_owners[:, None] == owner_codes[None, :]).astype(jnp.bfloat16)
    reader_rows = seq_rows.reshape(dp_count, seq_local)
    local_codes = jnp.arange(resident_adapters, dtype=jnp.int32) + my_index * resident_adapters
    wanted = (reader_rows[:, :, None] == local_codes[None, None, :]).astype(jnp.float32)
    serve_table = jnp.sum(wanted, axis=1).astype(jnp.bfloat16)
    usage_count = jnp.sum(wanted, axis=(0, 1))
    inverse_use = 1.0 / jnp.maximum(usage_count, 1.0)
    down_flattened = adapter_down_weight.reshape(resident_adapters, rank_span * block_span)
    up_flattened = adapter_up_weight.reshape(resident_adapters, rank_span * output_block)
    send_down = jnp.dot(serve_table, down_flattened, preferred_element_type=jnp.float32).astype(
        jnp.bfloat16
    )
    send_up = jnp.dot(serve_table, up_flattened, preferred_element_type=jnp.float32).astype(
        jnp.bfloat16
    )
    came_down, came_up = (
        lax.all_to_all(send_down, "dp", split_axis=0, concat_axis=0, tiled=True),
        lax.all_to_all(send_up, "dp", split_axis=0, concat_axis=0, tiled=True),
    )
    got_down = jnp.dot(from_owner, came_down, preferred_element_type=jnp.float32)
    got_up = jnp.dot(from_owner, came_up, preferred_element_type=jnp.float32)
    storage_down = got_down.astype(jnp.bfloat16).reshape(seq_local, rank_span, block_span)
    storage_up = got_up.astype(jnp.bfloat16).reshape(seq_local, rank_span, output_block)
    token_sequences = tokens.reshape(seq_local, seq_length, block_span)
    cot_seqs = cotangent.reshape(seq_local, seq_length, output_block)
    inner_part = jnp.einsum(
        "jby,jcy->jbc", token_sequences, storage_down, preferred_element_type=jnp.float32
    )
    back_part = jnp.einsum("slo,sro->slr", cot_seqs, storage_up, preferred_element_type=jnp.float32)
    joined = lax.psum(
        jnp.concatenate([inner_part, back_part], axis=2).astype(jnp.bfloat16), "tensor"
    ).astype(jnp.float32)
    middle_round = joined[:, :, :rank_span].astype(jnp.bfloat16)
    backward_round = joined[:, :, rank_span:].astype(jnp.bfloat16)
    partial_value = jnp.dot(tokens, key_value_weight, preferred_element_type=jnp.float32)
    frozen_backbone = lax.psum_scatter(
        partial_value.astype(jnp.bfloat16), "tensor", scatter_dimension=1, tiled=True
    ).astype(jnp.float32)
    adapter_output = jnp.einsum(
        "ivq,iqg->ivg", middle_round, storage_up, preferred_element_type=jnp.float32
    )
    key_value_output = (
        frozen_backbone + adapter_scale * adapter_output.reshape(token_row_matrix, output_block)
    ).astype(jnp.bfloat16)
    base_gradient = lax.dot_general(
        lax.all_gather(cotangent, "tensor", axis=1, tiled=True),
        key_value_weight,
        (((1,), (1,)), ((), ())),
        preferred_element_type=jnp.float32,
    )
    adapter_gradient = jnp.einsum(
        "cun,cny->cuy", backward_round, storage_down, preferred_element_type=jnp.float32
    )
    token_gradient = (
        base_gradient + adapter_scale * adapter_gradient.reshape(token_row_matrix, block_span)
    ).astype(jnp.bfloat16)
    down_term = (
        adapter_scale
        * jnp.einsum(
            "cfj,cfh->cjh", backward_round, token_sequences, preferred_element_type=jnp.float32
        )
    ).astype(jnp.bfloat16)
    up_term = (
        adapter_scale
        * jnp.einsum("slr,slo->sro", middle_round, cot_seqs, preferred_element_type=jnp.float32)
    ).astype(jnp.bfloat16)
    to_owner = from_owner.T
    ship_down = jnp.dot(
        to_owner, down_term.reshape(seq_local, -1), preferred_element_type=jnp.float32
    ).astype(jnp.bfloat16)
    ship_up = jnp.dot(
        to_owner, up_term.reshape(seq_local, -1), preferred_element_type=jnp.float32
    ).astype(jnp.bfloat16)
    back_down, back_up = (
        lax.all_to_all(ship_down, "dp", split_axis=0, concat_axis=0, tiled=True),
        lax.all_to_all(ship_up, "dp", split_axis=0, concat_axis=0, tiled=True),
    )
    serve_turned = serve_table.T
    grad_down = (
        jnp.dot(serve_turned, back_down, preferred_element_type=jnp.float32) * inverse_use[:, None]
    )
    grad_up = (
        jnp.dot(serve_turned, back_up, preferred_element_type=jnp.float32) * inverse_use[:, None]
    )
    grad_down = grad_down.reshape(resident_adapters, rank_span, block_span)
    grad_up = grad_up.reshape(resident_adapters, rank_span, output_block)
    return (key_value_output, token_gradient, grad_down, grad_up)


def solution(mesh):
    in_specs = (
        P("dp", "tensor"),
        P("tensor", None),
        P("dp", None, "tensor"),
        P("dp", None, "tensor"),
        P("dp", "tensor"),
        P(),
        P(),
    )
    out_specs = (
        P("dp", "tensor"),
        P("dp", "tensor"),
        P("dp", None, "tensor"),
        P("dp", None, "tensor"),
    )
    return jax.shard_map(
        on_device, mesh=mesh, in_specs=in_specs, out_specs=out_specs, check_vma=False
    )
```

profile of v0, /device:TPU:0, one launch (start us, length us, event | category | flops | bytes accessed | tf_op | source)
XLA Modules:
  0.0 199.3 jit_solution(10924035122615358659)
XLA Ops:
  8.2 1.2 copy.30
  11.4 1.2 reshape.74
  12.6 7.3 %all-to-all-start.1 = ((bf16[8,2,16384]{2,1,0:T(2,128)(2,1)}), bf16[8,2,16384]{2,1,0:T(2,128)(2,1)S(1)}, u32[]{:S(2)}, u32[]{:S(2)}) async-start(bf16[8,2,16384]{2,1,0:T(2,128)(2,1)} %reshape.74), calls=%async_computation.2 | async-start | bytes 1048576 | tf_op jit(solution)/shard_map/all_to_all | solution.py:51
  21.6 2.9 %reduce.1 = bf16[8,131072]{1,0:T(8,128)(2,1)} reduce(bf16[8,1,131072]{2,0,1:T(8,128)(2,1)S(1)} %fusion, bf16[]{:T(256)} %broadcast.29), dimensions={1}, to_apply=%copy.20.reduce_sub_computation | reduce | bytes 4194306 | tf_op jit(solution)/shard_map/all_to_all | solution.py:50
  24.5 4.7 %reshape.76 = bf16[8,2,65536]{2,1,0:T(2,128)(2,1)} reshape(bf16[8,131072]{1,0:T(8,128)(2,1)} %reduce.1) | data formatting | bytes 4194304
  29.3 5.1 %all-to-all-done.1 = bf16[8,2,16384]{2,1,0:T(2,128)(2,1)S(1)} async-done(((bf16[8,2,16384]{2,1,0:T(2,128)(2,1)}), bf16[8,2,16384]{2,1,0:T(2,128)(2,1)S(1)}, u32[]{:S(2)}, u32[]{:S(2)}) %all-to-all-start.1) | async-done | bytes 524320 | tf_op jit(solution)/shard_map/all_to_all | solution.py:51
  34.4 3.6 %all-to-all-start = ((bf16[8,2,65536]{2,1,0:T(2,128)(2,1)}), bf16[8,2,65536]{2,1,0:T(2,128)(2,1)S(1)}, u32[]{:S(2)}, u32[]{:S(2)}) async-start(bf16[8,2,65536]{2,1,0:T(2,128)(2,1)} %reshape.76), calls=%async_computation.1 | async-start | bytes 4194304 | tf_op jit(solution)/shard_map/all_to_all | solution.py:50
  38.1 1.8 reshape.75
  39.9 1.9 convolution_convert_fusion.5
  42.7 43.7 %all-to-all-done = bf16[8,2,65536]{2,1,0:T(2,128)(2,1)S(1)} async-done(((bf16[8,2,65536]{2,1,0:T(2,128)(2,1)}), bf16[8,2,65536]{2,1,0:T(2,128)(2,1)S(1)}, u32[]{:S(2)}, u32[]{:S(2)}) %all-to-all-start) | async-done | bytes 2097184 | tf_op jit(solution)/shard_map/all_to_all | solution.py:50
  86.4 4.4 %reshape.77 = bf16[8,1,131072]{2,1,0:T(2,128)(2,1)} reshape(bf16[8,2,65536]{2,1,0:T(2,128)(2,1)S(1)} %all-to-all-done) | data formatting | bytes 4194304
  90.8 4.7 %convolution_convert_fusion.2 = bf16[4,131072]{1,0:T(4,128)(2,1)S(1)} fusion(bf16[8,1,131072]{2,1,0:T(2,128)(2,1)} %reshape.77, s32[4]{0:T(128)S(1)} %and_select_fusion), kind=kOutput, calls=%fused_computation.5 | convolution fusion | flops 8912928 | bytes 3145744 | tf_op jit(solution)/shard_map/dot_general | solution.py:53
  97.3 10.3 %psum.7 = bf16[4,32,128]{2,1,0:T(8,128)(2,1)S(1)} all-reduce(bf16[4,32,128]{2,1,0:T(8,128)(2,1)S(1)} %pad_maximum_fusion), channel_id=1, replica_groups=mesh['dp'=8,'tensor'=4] {'tensor'}, use_global_device_ids=true, to_apply=%region_3.4 | all-reduce | flops 16384 | bytes 65536 | tf_op jit(solution)/shard_map/psum | solution.py:63
  109.5 1.2 reshape.80
  110.7 4.8 %all-to-all-start.3 = ((bf16[8,2,16384]{2,1,0:T(2,128)(2,1)}), bf16[8,2,16384]{2,1,0:T(2,128)(2,1)S(1)}, u32[]{:S(2)}, u32[]{:S(2)}) async-start(bf16[8,2,16384]{2,1,0:T(2,128)(2,1)} %reshape.80), calls=%async_computation.4 | async-start | bytes 1048576 | tf_op jit(solution)/shard_map/all_to_all | solution.py:109
  116.8 1.2 fusion.1
  118.0 2.9 %reduce.2 = bf16[8,131072]{1,0:T(8,128)(2,1)} reduce(bf16[8,1,131072]{2,0,1:T(8,128)(2,1)S(1)} %fusion.1, bf16[]{:T(256)} %broadcast.29), dimensions={1}, to_apply=%copy.22.reduce_sub_computation | reduce | bytes 4194306 | tf_op jit(solution)/shard_map/all_to_all | solution.py:108
  120.9 4.8 %reshape.78 = bf16[8,2,65536]{2,1,0:T(2,128)(2,1)} reshape(bf16[8,131072]{1,0:T(8,128)(2,1)} %reduce.2) | data formatting | bytes 4194304
  125.7 3.5 %all-to-all-done.3 = bf16[8,2,16384]{2,1,0:T(2,128)(2,1)S(1)} async-done(((bf16[8,2,16384]{2,1,0:T(2,128)(2,1)}), bf16[8,2,16384]{2,1,0:T(2,128)(2,1)S(1)}, u32[]{:S(2)}, u32[]{:S(2)}) %all-to-all-start.3) | async-done | bytes 524320 | tf_op jit(solution)/shard_map/all_to_all | solution.py:109
  130.0 3.6 %all-to-all-start.2 = ((bf16[8,2,65536]{2,1,0:T(2,128)(2,1)}), bf16[8,2,65536]{2,1,0:T(2,128)(2,1)S(1)}, u32[]{:S(2)}, u32[]{:S(2)}) async-start(bf16[8,2,65536]{2,1,0:T(2,128)(2,1)} %reshape.78), calls=%async_computation.3 | async-start | bytes 4194304 | tf_op jit(solution)/shard_map/all_to_all | solution.py:108
  133.7 5.4 %convolution_convert_fusion.6 = bf16[128,2048]{1,0:T(8,128)(2,1)} fusion(bf16[128,2048]{1,0:T(8,128)(2,1)S(1)} %copy-done, bf16[2048,2048]{1,0:T(8,128)(2,1)} %param.8), kind=kOutput, calls=%fused_computation.17 | convolution fusion | flops 1074003968 | bytes 9437184 | tf_op jit(solution)/shard_map/dot_general | solution.py:68
  139.2 7.2 %all_gather.3 = bf16[128,2048]{1,0:T(8,128)(2,1)S(1)} all-gather(bf16[128,512]{1,0:T(8,128)(2,1)S(1)} %copy-done.5), channel_id=1, replica_groups=mesh['dp'=8,'tensor'=4] {'tensor'}, dimensions={1}, use_global_device_ids=true | all-gather | bytes 655360 | tf_op jit(solution)/shard_map/all_gather | solution.py:79
  147.5 14.9 %reduce-scatter.2.cloned.1.call-done = bf16[128,512]{1,0:T(8,128)(2,1)} async-done(((bf16[128,2048]{1,0:T(8,128)(2,1)}), bf16[128,512]{1,0:T(8,128)(2,1)}) %reduce-scatter.2.cloned.1.call-update) | async-done | bytes 131088 | tf_op jit(solution)/shard_map/reduce_scatter | solution.py:69
  162.4 1.6 fusion.25
  164.0 2.6 %convolution_multiply_fusion.3 = f32[4,32,2048]{2,1,0:T(8,128)S(1)} fusion(bf16[1,4,64,2048]{3,1,2,0:T(4,128)(2,1)} %bitcast.83, bf16[4,32,128]{2,1,0:T(8,128)(2,1)S(1)} %psum.7), kind=kOutput, calls=%fused_computation.15 | convolution fusion | flops 33816576 | bytes 2129920 | tf_op jit(solution)/shard_map/cun,cny->cuy/dot_general | solution.py:84
  166.6 7.1 %fusion.6 = bf16[128,2048]{1,0:T(8,128)(2,1)} fusion(f32[128,2048]{1,0:T(8,128)S(1)} %bitcast.80, bf16[128,2048]{1,0:T(8,128)(2,1)S(1)} %all_gather.3, bf16[2048,2048]{1,0:T(8,128)(2,1)} %param.8), kind=kOutput, calls=%fused_computation.18 | convolution fusion | flops 1074266112 | bytes 10485760 | tf_op jit(solution)/shard_map/dot_general | solution.py:78
  173.6 3.5 %reshape.81 = bf16[8,1,32768]{2,1,0:T(2,128)(2,1)} reshape(bf16[8,2,16384]{2,1,0:T(2,128)(2,1)} %copy-done.2) | data formatting | bytes 1048576
  177.1 1.9 convolution_multiply_fusion.1
  179.9 1.5 all-to-all-done.2
  181.4 4.4 %reshape.79 = bf16[8,1,131072]{2,1,0:T(2,128)(2,1)} reshape(bf16[8,2,65536]{2,1,0:T(2,128)(2,1)S(1)} %all-to-all-done.2) | data formatting | bytes 4194304
  185.8 4.7 %convolution_multiply_fusion = f32[3,131072]{1,0:T(4,128)S(1)} fusion(bf16[8,3]{0,1:T(4,128)(2,1)S(1)} %get-tuple-element.5, bf16[8,1,131072]{2,1,0:T(2,128)(2,1)} %reshape.79, f32[3]{0:T(128)S(1)} %maximum_divide_fusion), kind=kOutput, calls=%fused_computation.2 | convolution fusion | flops 6684672 | bytes 3670076 | tf_op jit(solution)/shard_map/dot_general | solution.py:113
  190.4 2.1 %copy.70 = f32[1,3,64,2048]{3,2,1,0:T(8,128)} copy(f32[1,3,64,2048]{3,1,2,0:T(4,128)S(1)} %bitcast.79) | data formatting | bytes 3145728
  (37 shorter events, 13.7 us)
Async XLA Ops:
  7.2 88.3 %copy-start = (bf16[128,2048]{1,0:T(8,128)(2,1)S(1)}, bf16[128,2048]{1,0:T(8,128)(2,1)}, u32[]{:S(2)}) copy-start(bf16[128,2048]{1,0:T(8,128)(2,1)} %param.7) | copy-start | bytes 1572868
  8.2 11.7 %copy-start.4 = (bf16[3,64,2048]{2,1,0:T(8,128)(2,1)S(1)}, bf16[3,64,2048]{2,1,0:T(8,128)(2,1)}, u32[]{:S(2)}) copy-start(bf16[3,64,2048]{2,1,0:T(8,128)(2,1)} %param.9) | copy-start | bytes 2359300
  12.6 21.8 %all-to-all-start.1 = ((bf16[8,2,16384]{2,1,0:T(2,128)(2,1)}), bf16[8,2,16384]{2,1,0:T(2,128)(2,1)S(1)}, u32[]{:S(2)}, u32[]{:S(2)}) async-start(bf16[8,2,16384]{2,1,0:T(2,128)(2,1)} %reshape.74), calls=%async_computation.2 | async-start | bytes 1048576 | tf_op jit(solution)/shard_map/all_to_all | solution.py:51
  34.4 52.1 %all-to-all-start = ((bf16[8,2,65536]{2,1,0:T(2,128)(2,1)}), bf16[8,2,65536]{2,1,0:T(2,128)(2,1)S(1)}, u32[]{:S(2)}, u32[]{:S(2)}) async-start(bf16[8,2,65536]{2,1,0:T(2,128)(2,1)} %reshape.76), calls=%async_computation.1 | async-start | bytes 4194304 | tf_op jit(solution)/shard_map/all_to_all | solution.py:50
  38.0 4.5 %copy-start.5 = (bf16[128,512]{1,0:T(8,128)(2,1)S(1)}, bf16[128,512]{1,0:T(8,128)(2,1)}, u32[]{:S(2)}) copy-start(bf16[128,512]{1,0:T(8,128)(2,1)} %param.11) | copy-start | bytes 393220
  41.8 0.7 copy-start.3
  95.5 1.0 copy-start.1
  110.7 18.5 %all-to-all-start.3 = ((bf16[8,2,16384]{2,1,0:T(2,128)(2,1)}), bf16[8,2,16384]{2,1,0:T(2,128)(2,1)S(1)}, u32[]{:S(2)}, u32[]{:S(2)}) async-start(bf16[8,2,16384]{2,1,0:T(2,128)(2,1)} %reshape.80), calls=%async_computation.4 | async-start | bytes 1048576 | tf_op jit(solution)/shard_map/all_to_all | solution.py:109
  129.2 0.8 copy-start.2
  130.0 51.3 %all-to-all-start.2 = ((bf16[8,2,65536]{2,1,0:T(2,128)(2,1)}), bf16[8,2,65536]{2,1,0:T(2,128)(2,1)S(1)}, u32[]{:S(2)}, u32[]{:S(2)}) async-start(bf16[8,2,65536]{2,1,0:T(2,128)(2,1)} %reshape.78), calls=%async_computation.3 | async-start | bytes 4194304 | tf_op jit(solution)/shard_map/all_to_all | solution.py:108
  133.7 28.7 %reduce-scatter.2.cloned.1.call-start = ((), (), s32[]{:S(2)}) async-start(), calls=%async_computation.5 | async-start | bytes 655360 | tf_op jit(solution)/shard_map/reduce_scatter | solution.py:69
Sparse Core Ops, SparseCore 0:
  139.3 23.0 reduce-scatter.1
where the time goes:
time: 200 us; the launch traced here: 199 us
  waiting for transfers between devices  68.7 us (34%)
  local copies, waits for them, and re-layouts  34.9 us (17%)
  matrix products  34.1 us (17%)
  starting transfers between devices  19.3 us (10%)
  blocking collectives  17.5 us (9%)
  between operations  14.2 us (7%)
  other arithmetic  10.6 us (5%)
    all_to_all x1, waiting for transfers between devices, on_device(): lax.all_to_all(send_down, 'dp', split_axis=0, concat_axis=0, tiled=True)  43.7 us
    unnamed x26, local copies, waits for them, and re-layouts  34.2 us
    reduce_scatter x1, waiting for transfers between devices, on_device(): lax.psum_scatter(partial_value.astype(jnp.bfloat16), 'tensor', scatter_di...  14.9 us
    psum x1, blocking collectives, on_device(): lax.psum(jnp.concatenate([inner_part, back_part], axis=2).astype(jnp.bflo...  10.3 us
    all_to_all x1, starting transfers between devices, on_device(): lax.all_to_all(send_up, 'dp', split_axis=0, concat_axis=0, tiled=True)  7.28 us
    all_gather x1, blocking collectives, on_device(): lax.all_gather(cotangent, 'tensor', axis=1, tiled=True)  7.21 us
    dot_general x1, matrix products, on_device(): lax.dot_general(lax.all_gather(cotangent, 'tensor', axis=1, tiled=True),...  7.08 us
    dot_general x1, matrix products, on_device(): jnp.dot(tokens, key_value_weight, preferred_element_type=jnp.float32)  5.44 us
  transfers between devices with their start and end apart: 5, of which 5 were waited for; matrix products, arithmetic and copies ran while one was open for 24% of the time, Pallas kernels for 0%

commit v1 on v0

v1 whole, which is shorter than its diff:
```python
import functools

import jax
import jax.numpy as jnp
from jax import lax
from jax.experimental import pallas as pl
from jax.experimental.pallas import tpu as pltpu
from jax.sharding import PartitionSpec as P

adapter_scale = 0.25
MESH = pl.DeviceIdType.MESH
F32 = jnp.float32
BF16 = jnp.bfloat16


def nt_dot(a, b):
    return lax.dot_general(a, b, (((1,), (1,)), ((), ())), preferred_element_type=F32)


def tn_dot(a, b):
    return lax.dot_general(a, b, (((0,), (0,)), ((), ())), preferred_element_type=F32)


def routes(dp_count, seqs, resident, seq_ref, store_ref, table_ref, weight_ref):
    d = lax.axis_index("dp")
    rows = [store_ref[seq_ref[d * seqs + j]] for j in range(seqs)]
    dist = [lax.rem(lax.div(r, jnp.int32(resident)) + dp_count - d, dp_count) for r in rows]
    for j in range(seqs):
        table_ref[2 * dp_count + j] = dist[j]
    for k in range(dp_count):
        pick = jnp.int32(0)
        for j in range(seqs):
            pick = jnp.where(dist[j] == k, jnp.int32(j), pick)
        table_ref[k] = pick
    counts = [jnp.float32(0.0)] * resident
    for k in range(dp_count):
        reader = lax.rem(d + dp_count - k, dp_count)
        found = jnp.int32(-1)
        for j in range(seqs):
            local = store_ref[seq_ref[reader * seqs + j]] - d * resident
            found = jnp.where((local >= 0) & (local < resident), local, found)
        table_ref[dp_count + k] = jnp.maximum(found, 0)
        for a in range(resident):
            hit = jnp.where(found == a, jnp.float32(1.0), jnp.float32(0.0))
            weight_ref[a * dp_count + k] = hit
            counts[a] = counts[a] + hit
    for a in range(resident):
        weight_ref[resident * dp_count + a] = counts[a]


def kernel(
    dp_count,
    tensor_count,
    groups,
    table_ref,
    weight_ref,
    tok_ref,
    w_ref,
    down_ref,
    up_ref,
    cot_ref,
    cot_seq_ref,
    kvo_ref,
    tg_ref,
    gd_ref,
    gu_ref,
    w_v,
    slot_out,
    slot_in,
    ret_out,
    ret_in,
    cots,
    parts,
    part_in,
    ranks,
    back_m,
    inner_m,
    acc,
    w_sem,
    slot_ssem,
    slot_rsem,
    ret_ssem,
    ret_rsem,
    cot_ssem,
    cot_rsem,
    part_ssem,
    part_rsem,
    rank_ssem,
    rank_rsem,
):
    d = lax.axis_index("dp")
    t = lax.axis_index("tensor")
    resident, rank, block = down_ref.shape
    out_block = up_ref.shape[2]
    seqs, length = tok_ref.shape[:2]
    rows = seqs * length
    per_group = dp_count // groups

    def dp_to(k):
        return lax.rem(d + k, dp_count)

    def dp_from(k):
        return lax.rem(d + dp_count - k, dp_count)

    def t_to(q):
        return lax.rem(t + q, tensor_count)

    def t_from(q):
        return lax.rem(t + tensor_count - q, tensor_count)

    def w_copy(i):
        c = t_to(i)
        return pltpu.make_async_copy(
            w_ref.at[:, pl.ds(pl.multiple_of(c * out_block, out_block), out_block)],
            w_v.at[i],
            w_sem.at[i],
        )

    for i in range(tensor_count):
        w_copy(i).start()

    barrier = pltpu.get_barrier_semaphore()
    for k in range(1, dp_count):
        pl.semaphore_signal(barrier, inc=1, device_id={"dp": dp_to(k)}, device_id_type=MESH)
    for q in range(1, tensor_count):
        pl.semaphore_signal(barrier, inc=1, device_id={"tensor": t_to(q)}, device_id_type=MESH)

    for k in range(dp_count):
        pick = table_ref[k]
        target = slot_in if k == 0 else slot_out
        target[k * length:(k + 1) * length, :block] = tok_ref[pick]
        target[k * length:(k + 1) * length, block:] = cot_seq_ref[pick]

    pl.semaphore_wait(barrier, dp_count + tensor_count - 2)

    def cot_copy(q):
        return pltpu.make_async_remote_copy(
            cot_ref, cots.at[q], cot_ssem.at[q], cot_rsem.at[q],
            device_id={"tensor": t_to(q)}, device_id_type=MESH)

    def slot_copy(k):
        at = pl.ds(k * length, length)
        return pltpu.make_async_remote_copy(
            slot_out.at[at], slot_in.at[at], slot_ssem.at[k], slot_rsem.at[k],
            device_id={"dp": dp_to(k)}, device_id_type=MESH)

    def ret_copy(k):
        return pltpu.make_async_remote_copy(
            ret_out.at[k], ret_in.at[k], ret_ssem.at[k], ret_rsem.at[k],
            device_id={"dp": dp_from(k)}, device_id_type=MESH)

    def part_copy(q):
        return pltpu.make_async_remote_copy(
            parts.at[q], part_in.at[q], part_ssem.at[q], part_rsem.at[q],
            device_id={"tensor": t_to(q)}, device_id_type=MESH)

    def rank_copy(g, q):
        return pltpu.make_async_remote_copy(
            ranks.at[g, t], ranks.at[g, t], rank_ssem.at[g, q], rank_rsem.at[g, q],
            device_id={"tensor": t_to(q)}, device_id_type=MESH)

    for k in range(1, dp_count):
        slot_copy(k).start()
    for q in range(1, tensor_count):
        cot_copy(q).start()

    adapter_of = [table_ref[dp_count + k] for k in range(dp_count)]
    weights = [[weight_ref[a * dp_count + k] for k in range(dp_count)] for a in range(resident)]
    counts = [weight_ref[resident * dp_count + a] for a in range(resident)]

    def frozen_block(i, carry):
        w_copy(i).wait()
        parts[i] = jnp.dot(tok_ref[...].reshape(rows, block), w_v[i], preferred_element_type=F32).astype(BF16)
        return carry

    lax.fori_loop(0, tensor_count, frozen_block, 0)

    def rank_stage(g):
        for m in range(per_group):
            k = g * per_group + m
            if k:
                slot_copy(k).wait_recv()
            x = slot_in[k * length:(k + 1) * length, :block]
            c = slot_in[k * length:(k + 1) * length, block:]
            inner = nt_dot(x, down_ref[adapter_of[k]])
            back = nt_dot(c, up_ref[adapter_of[k]])
            ranks[g, t, m * length:(m + 1) * length, :] = jnp.concatenate(
                [inner, back], axis=1).astype(BF16)
        for q in range(1, tensor_count):
            rank_copy(g, q).start()

    def base_block(i, carry):
        q = lax.rem(tensor_count - i, tensor_count)
        acc[...] += nt_dot(cots[q], w_v[i])
        return carry

    def use_stage(g):
        for q in range(1, tensor_count):
            s = t_from(q)
            pltpu.make_async_remote_copy(
                ranks.at[g, s], ranks.at[g, s], rank_ssem.at[g, q], rank_rsem.at[g, q],
                device_id={"tensor": t_to(q)}, device_id_type=MESH).wait_recv()
        for q in range(1, tensor_count):
            rank_copy(g, q).wait_send()
        total = ranks[g, 0].astype(F32)
        for s in range(1, tensor_count):
            total = total + ranks[g, s].astype(F32)
        for m in range(per_group):
            k = g * per_group + m
            lines = total[m * length:(m + 1) * length]
            inner = lines[:, :rank].astype(BF16)
            back = lines[:, rank:].astype(BF16)
            target = ret_out if k else ret_in
            target[k, :, :block] = (adapter_scale * jnp.dot(
                back, down_ref[adapter_of[k]], preferred_element_type=F32)).astype(BF16)
            target[k, :, block:] = (adapter_scale * jnp.dot(
                inner, up_ref[adapter_of[k]], preferred_element_type=F32)).astype(BF16)
            for a in range(resident):
                at = slice(k * length, (k + 1) * length)
                back_m[a, at, :] = (back.astype(F32) * weights[a][k]).astype(BF16)
                inner_m[a, at, :] = (inner.astype(F32) * weights[a][k]).astype(BF16)
            if k:
                ret_copy(k).start()

    rank_stage(0)
    for q in range(1, tensor_count):
        part_copy(q).start()
    acc[...] = nt_dot(cot_ref[...], w_v[0])
    for q in range(1, tensor_count):
        cot_copy(q).wait_recv()
    half = max(1, tensor_count // 2)
    lax.fori_loop(1, half, base_block, 0)
    use_stage(0)
    for g in range(1, groups):
        rank_stage(g)
        if g == 1:
            lax.fori_loop(half, tensor_count, base_block, 0)
        use_stage(g)

    x_all = slot_in[:, :block]
    c_all = slot_in[:, block:]
    for a in range(resident):
        gd_ref[a] = tn_dot(back_m[a], x_all) * (
            adapter_scale / jnp.maximum(jnp.full((1, block), counts[a], F32), 1.0))
        gu_ref[a] = tn_dot(inner_m[a], c_all) * (
            adapter_scale / jnp.maximum(jnp.full((1, out_block), counts[a], F32), 1.0))

    for q in range(1, tensor_count):
        part_copy(q).wait_recv()
    backbone = parts[0].astype(F32)
    for q in range(1, tensor_count):
        backbone = backbone + part_in[q].astype(F32)
    for k in range(1, dp_count):
        ret_copy(k).wait_recv()
    for j in range(seqs):
        at = slice(j * length, (j + 1) * length)
        came = ret_in[table_ref[2 * dp_count + j]]
        kvo_ref[at, :] = (backbone[at] + came[:, block:].astype(F32)).astype(BF16)
        tg_ref[at, :] = (acc[at, :] + came[:, :block].astype(F32)).astype(BF16)

    for k in range(1, dp_count):
        slot_copy(k).wait_send()
        ret_copy(k).wait_send()
    for q in range(1, tensor_count):
        cot_copy(q).wait_send()
        part_copy(q).wait_send()


def on_device(dp_count, tensor_count, tok, w, down, up, cot, seq_index, storage):
    resident, rank, block = down.shape
    out_block = up.shape[2]
    rows = tok.shape[0]
    seqs = seq_index.shape[0] // dp_count
    length = rows // seqs
    groups = 2
    wide = block + out_block
    vmem = pl.BlockSpec(memory_space=pltpu.VMEM)
    smem = pl.BlockSpec(memory_space=pltpu.SMEM)
    dma = pltpu.SemaphoreType.DMA
    table, weights = pl.pallas_call(
        functools.partial(routes, dp_count, seqs, resident),
        out_shape=(
            jax.ShapeDtypeStruct((2 * dp_count + seqs,), jnp.int32),
            jax.ShapeDtypeStruct((resident * dp_count + resident,), F32),
        ),
        in_specs=[smem, smem],
        out_specs=(smem, smem),
    )(seq_index, storage)
    return pl.pallas_call(
        functools.partial(kernel, dp_count, tensor_count, groups),
        out_shape=(
            jax.ShapeDtypeStruct((rows, out_block), BF16),
            jax.ShapeDtypeStruct((rows, block), BF16),
            jax.ShapeDtypeStruct((resident, rank, block), F32),
            jax.ShapeDtypeStruct((resident, rank, out_block), F32),
        ),
        in_specs=[smem, smem, vmem, pl.BlockSpec(memory_space=pl.ANY), vmem, vmem, vmem, vmem],
        out_specs=(vmem, vmem, vmem, vmem),
        scratch_shapes=[
            pltpu.VMEM((tensor_count, w.shape[0], out_block), BF16),
            pltpu.VMEM((dp_count * length, wide), BF16),
            pltpu.VMEM((dp_count * length, wide), BF16),
            pltpu.VMEM((dp_count, length, wide), BF16),
            pltpu.VMEM((dp_count, length, wide), BF16),
            pltpu.VMEM((tensor_count, rows, out_block), BF16),
            pltpu.VMEM((tensor_count, rows, out_block), BF16),
            pltpu.VMEM((tensor_count, rows, out_block), BF16),
            pltpu.VMEM((groups, tensor_count, dp_count // groups * length, 2 * rank), BF16),
            pltpu.VMEM((resident, dp_count * length, rank), BF16),
            pltpu.VMEM((resident, dp_count * length, rank), BF16),
            pltpu.VMEM((rows, block), F32),
            dma((tensor_count,)),
            dma((dp_count,)),
            dma((dp_count,)),
            dma((dp_count,)),
            dma((dp_count,)),
            dma((tensor_count,)),
            dma((tensor_count,)),
            dma((tensor_count,)),
            dma((tensor_count,)),
            dma((groups, tensor_count)),
            dma((groups, tensor_count)),
        ],
        compiler_params=pltpu.CompilerParams(
            collective_id=0, has_side_effects=True, vmem_limit_bytes=60 * 1024 * 1024
        ),
    )(
        table, weights, tok.reshape(seqs, length, block), w, down, up, cot,
        cot.reshape(seqs, length, out_block))


def solution(mesh):
    in_specs = (
        P("dp", "tensor"),
        P("tensor", None),
        P("dp", None, "tensor"),
        P("dp", None, "tensor"),
        P("dp", "tensor"),
        P(),
        P(),
    )
    out_specs = (
        P("dp", "tensor"),
        P("dp", "tensor"),
        P("dp", None, "tensor"),
        P("dp", None, "tensor"),
    )
    return jax.shard_map(
        functools.partial(on_device, mesh.shape["dp"], mesh.shape["tensor"]),
        mesh=mesh, in_specs=in_specs, out_specs=out_specs, check_vma=False,
    )
```

time: 200 us -> 91 us (0.46)
  Pallas kernels: 0 us -> 83.2 us
  waiting for transfers between devices: 68.7 us -> 0 us
  matrix products: 34.1 us -> 0 us
  local copies, waits for them, and re-layouts: 34.9 us -> 6.95 us
  starting transfers between devices: 19.3 us -> 0 us
  blocking collectives: 17.5 us -> 0 us
  between operations: 14.2 us -> 0.65 us
  other arithmetic: 10.6 us -> 0 us
    pallas_call x0 -> x2, Pallas kernels: none -> 83.2 us  [the longest x1 81.8 us: on_device(): pl.pallas_call(functools.partial(kernel, dp_count, tensor_count, groups),...]
    all_to_all x4 -> x0, waiting for transfers between devices: 53.8 us -> none  [the longest x1 43.7 us: on_device(): lax.all_to_all(send_down, 'dp', split_axis=0, concat_axis=0, tiled=True)]
    dot_general x16 -> x0, matrix products: 34.1 us -> none  [the longest x1 7.08 us: on_device(): lax.dot_general(lax.all_gather(cotangent, 'tensor', axis=1, tiled=True),...]
    unnamed x26 -> x6, local copies, waits for them, and re-layouts: 34.2 us -> 6.95 us
    all_to_all x4 -> x0, starting transfers between devices: 19.3 us -> none  [the longest x1 7.28 us: on_device(): lax.all_to_all(send_up, 'dp', split_axis=0, concat_axis=0, tiled=True)]
    reduce_scatter x1 -> x0, waiting for transfers between devices: 14.9 us -> none  [on_device(): lax.psum_scatter(partial_value.astype(jnp.bfloat16), 'tensor', scatter_di...]
    psum x1 -> x0, blocking collectives: 10.3 us -> none  [on_device(): lax.psum(jnp.concatenate([inner_part, back_part], axis=2).astype(jnp.bflo...]
    all_to_all x4 -> x0, other arithmetic: 7.84 us -> none  [the longest x1 2.93 us: on_device(): lax.all_to_all(send_down, 'dp', split_axis=0, concat_axis=0, tiled=True)]
  transfers between devices with their start and end apart: 5 -> 0, of which waited for: 5 -> 0; matrix products, arithmetic and copies ran while one was open for 24% -> 0% of each run, Pallas kernels for 0% -> 0%
where the time goes in v1:
time: 91 us; the launch traced here: 90.8 us
  Pallas kernels  83.2 us (91%)
  local copies, waits for them, and re-layouts  6.95 us (8%)
    pallas_call x1, Pallas kernels, on_device(): pl.pallas_call(functools.partial(kernel, dp_count, tensor_count, groups),...  81.8 us
    unnamed x6, local copies, waits for them, and re-layouts  6.95 us

profile of v1, /device:TPU:0, one launch (start us, length us, event | category | flops | bytes accessed | tf_op | source)
XLA Modules:
  0.0 90.8 jit_solution(15704406842952903855)
XLA Ops:
  0.6 1.4 %shard_map.102 = (s32[20]{0:T(128)}, f32[27]{0:T(128)}) custom-call(s32[32]{0:T(128)} %seq_ref.1, s32[24]{0:T(128)} %store_ref.1), custom_call_target="tpu_custom_call" | custom-call | tf_op jit(solution)/shard_map/pallas_call | solution.py:280
  2.0 81.8 %shard_map.103 = (bf16[128,512]{1,0:T(8,128)(2,1)}, bf16[128,2048]{1,0:T(8,128)(2,1)}, f32[3,64,2048]{2,1,0:T(8,128)}, f32[3,64,512]{2,1,0:T(8,128)}) custom-call(s32[20]{0:T(128)} %get-tuple-element.6.table_ref, f32[27]{0:T(128)} %get-tuple-element.7.weight_ref, bf16[4,32,2048]{2,1,0:T(8,128)(2,1)} %bitcast.3, bf16[2048,2048]{1,0:T(8,128)(2,1)} %w_ref.1, ...), custom_call_target="tpu_custom_call" | custom-call | tf_op jit(solution)/shard_map/pallas_call | solution.py:289
  83.8 1.6 %copy.15 = bf16[128,512]{1,0:T(8,128)(2,1)} copy(bf16[128,512]{1,0:T(8,128)(2,1)} %get-tuple-element.12) | data formatting | bytes 262144
  85.4 1.9 %copy.16 = bf16[128,2048]{1,0:T(8,128)(2,1)} copy(bf16[128,2048]{1,0:T(8,128)(2,1)} %get-tuple-element.13) | data formatting | bytes 1048576
  87.2 0.0 copy-start
  87.2 2.8 %copy.17 = f32[3,64,2048]{2,1,0:T(8,128)} copy(f32[3,64,2048]{2,1,0:T(8,128)} %get-tuple-element.14) | data formatting | bytes 3145728
  90.0 0.0 copy-done
  90.0 0.7 copy.18
Async XLA Ops:
  87.2 2.8 %copy-start = (f32[3,64,512]{2,1,0:T(8,128)S(1)}, f32[3,64,512]{2,1,0:T(8,128)}, u32[]{:S(2)}) copy-start(f32[3,64,512]{2,1,0:T(8,128)} %get-tuple-element.15) | copy-start | bytes 1179652

commit v2 on v1

--- a/solution.py
+++ b/solution.py
@@ -21,10 +21,25 @@
     return lax.dot_general(a, b, (((0,), (0,)), ((), ())), preferred_element_type=F32)
 
 
+def partner(d, k, dp_count):
+    out, bit = d, 1
+    while bit < dp_count:
+        if k & bit:
+            out = out + bit - 2 * bit * lax.rem(lax.div(d, jnp.int32(bit)), jnp.int32(2))
+        bit *= 2
+    return out
+
+
 def routes(dp_count, seqs, resident, seq_ref, store_ref, table_ref, weight_ref):
     d = lax.axis_index("dp")
     rows = [store_ref[seq_ref[d * seqs + j]] for j in range(seqs)]
-    dist = [lax.rem(lax.div(r, jnp.int32(resident)) + dp_count - d, dp_count) for r in rows]
+    owners = [lax.div(r, jnp.int32(resident)) for r in rows]
+    dist = []
+    for j in range(seqs):
+        slot = jnp.int32(0)
+        for k in range(1, dp_count):
+            slot = jnp.where(owners[j] == partner(d, k, dp_count), jnp.int32(k), slot)
+        dist.append(slot)
     for j in range(seqs):
         table_ref[2 * dp_count + j] = dist[j]
     for k in range(dp_count):
@@ -34,7 +49,7 @@
         table_ref[k] = pick
     counts = [jnp.float32(0.0)] * resident
     for k in range(dp_count):
-        reader = lax.rem(d + dp_count - k, dp_count)
+        reader = partner(d, k, dp_count)
         found = jnp.int32(-1)
         for j in range(seqs):
             local = store_ref[seq_ref[reader * seqs + j]] - d * resident
@@ -48,20 +63,29 @@
         weight_ref[resident * dp_count + a] = counts[a]
 
 
+def slot_groups(dp_count):
+    order = list(range(dp_count - 1, -1, -1))
+    quarter = dp_count // 4
+    return [order[:quarter], order[quarter:2 * quarter], order[2 * quarter:]]
+
+
 def kernel(
     dp_count,
     tensor_count,
-    groups,
     table_ref,
     weight_ref,
     tok_ref,
     w_ref,
-    down_ref,
-    up_ref,
+    down_hbm,
+    up_hbm,
     cot_ref,
     cot_seq_ref,
     kvo_ref,
     tg_ref,
+    gd_hbm,
+    gu_hbm,
+    down_ref,
+    up_ref,
     gd_ref,
     gu_ref,
     w_v,
@@ -77,6 +101,7 @@
     inner_m,
     acc,
     w_sem,
+    local_sem,
     slot_ssem,
     slot_rsem,
     ret_ssem,
@@ -94,13 +119,11 @@
     out_block = up_ref.shape[2]
     seqs, length = tok_ref.shape[:2]
     rows = seqs * length
-    per_group = dp_count // groups
+    groups = slot_groups(dp_count)
+    starts = [sum(len(g) for g in groups[:i]) for i in range(len(groups))]
 
     def dp_to(k):
-        return lax.rem(d + k, dp_count)
-
-    def dp_from(k):
-        return lax.rem(d + dp_count - k, dp_count)
+        return partner(d, k, dp_count)
 
     def t_to(q):
         return lax.rem(t + q, tensor_count)
@@ -116,8 +139,14 @@
             w_sem.at[i],
         )
 
+    down_copy = pltpu.make_async_copy(down_hbm, down_ref, local_sem.at[0])
+    up_copy = pltpu.make_async_copy(up_hbm, up_ref, local_sem.at[1])
+    gd_copy = pltpu.make_async_copy(gd_ref, gd_hbm, local_sem.at[2])
+    gu_copy = pltpu.make_async_copy(gu_ref, gu_hbm, local_sem.at[3])
     for i in range(tensor_count):
         w_copy(i).start()
+    down_copy.start()
+    up_copy.start()
 
     barrier = pltpu.get_barrier_semaphore()
     for k in range(1, dp_count):
@@ -147,19 +176,22 @@
     def ret_copy(k):
         return pltpu.make_async_remote_copy(
             ret_out.at[k], ret_in.at[k], ret_ssem.at[k], ret_rsem.at[k],
-            device_id={"dp": dp_from(k)}, device_id_type=MESH)
+            device_id={"dp": dp_to(k)}, device_id_type=MESH)
 
     def part_copy(q):
         return pltpu.make_async_remote_copy(
             parts.at[q], part_in.at[q], part_ssem.at[q], part_rsem.at[q],
             device_id={"tensor": t_to(q)}, device_id_type=MESH)
 
+    def rank_rows(g):
+        return pl.ds(starts[g] * length, len(groups[g]) * length)
+
     def rank_copy(g, q):
         return pltpu.make_async_remote_copy(
-            ranks.at[g, t], ranks.at[g, t], rank_ssem.at[g, q], rank_rsem.at[g, q],
+            ranks.at[t, rank_rows(g)], ranks.at[t, rank_rows(g)], rank_ssem.at[g, q], rank_rsem.at[g, q],
             device_id={"tensor": t_to(q)}, device_id_type=MESH)
 
-    for k in range(1, dp_count):
+    for k in range(dp_count - 1, 0, -1):
         slot_copy(k).start()
     for q in range(1, tensor_count):
         cot_copy(q).start()
@@ -176,15 +208,14 @@
     lax.fori_loop(0, tensor_count, frozen_block, 0)
 
     def rank_stage(g):
-        for m in range(per_group):
-            k = g * per_group + m
+        for m, k in enumerate(groups[g]):
             if k:
                 slot_copy(k).wait_recv()
             x = slot_in[k * length:(k + 1) * length, :block]
             c = slot_in[k * length:(k + 1) * length, block:]
             inner = nt_dot(x, down_ref[adapter_of[k]])
             back = nt_dot(c, up_ref[adapter_of[k]])
-            ranks[g, t, m * length:(m + 1) * length, :] = jnp.concatenate(
+            ranks[t, (starts[g] + m) * length:(starts[g] + m + 1) * length, :] = jnp.concatenate(
                 [inner, back], axis=1).astype(BF16)
         for q in range(1, tensor_count):
             rank_copy(g, q).start()
@@ -198,15 +229,14 @@
         for q in range(1, tensor_count):
             s = t_from(q)
             pltpu.make_async_remote_copy(
-                ranks.at[g, s], ranks.at[g, s], rank_ssem.at[g, q], rank_rsem.at[g, q],
+                ranks.at[s, rank_rows(g)], ranks.at[s, rank_rows(g)], rank_ssem.at[g, q], rank_rsem.at[g, q],
                 device_id={"tensor": t_to(q)}, device_id_type=MESH).wait_recv()
         for q in range(1, tensor_count):
             rank_copy(g, q).wait_send()
-        total = ranks[g, 0].astype(F32)
+        total = ranks[0, rank_rows(g)].astype(F32)
         for s in range(1, tensor_count):
-            total = total + ranks[g, s].astype(F32)
-        for m in range(per_group):
-            k = g * per_group + m
+            total = total + ranks[s, rank_rows(g)].astype(F32)
+        for m, k in enumerate(groups[g]):
             lines = total[m * length:(m + 1) * length]
             inner = lines[:, :rank].astype(BF16)
             back = lines[:, rank:].astype(BF16)
@@ -222,20 +252,22 @@
             if k:
                 ret_copy(k).start()
 
+    for q in range(1, tensor_count):
+        part_copy(q).start()
+    half = max(1, tensor_count // 2)
+    acc[...] = nt_dot(cot_ref[...], w_v[0])
+    for q in range(1, tensor_count):
+        cot_copy(q).wait_recv()
+    lax.fori_loop(1, half, base_block, 0)
+    down_copy.wait()
+    up_copy.wait()
     rank_stage(0)
-    for q in range(1, tensor_count):
-        part_copy(q).start()
-    acc[...] = nt_dot(cot_ref[...], w_v[0])
-    for q in range(1, tensor_count):
-        cot_copy(q).wait_recv()
-    half = max(1, tensor_count // 2)
-    lax.fori_loop(1, half, base_block, 0)
+    lax.fori_loop(half, tensor_count, base_block, 0)
     use_stage(0)
-    for g in range(1, groups):
-        rank_stage(g)
-        if g == 1:
-            lax.fori_loop(half, tensor_count, base_block, 0)
-        use_stage(g)
+    rank_stage(1)
+    use_stage(1)
+    rank_stage(2)
+    use_stage(2)
 
     x_all = slot_in[:, :block]
     c_all = slot_in[:, block:]
@@ -245,6 +277,8 @@
         gu_ref[a] = tn_dot(inner_m[a], c_all) * (
             adapter_scale / jnp.maximum(jnp.full((1, out_block), counts[a], F32), 1.0))
 
+    gd_copy.start()
+    gu_copy.start()
     for q in range(1, tensor_count):
         part_copy(q).wait_recv()
     backbone = parts[0].astype(F32)
@@ -264,6 +298,28 @@
     for q in range(1, tensor_count):
         cot_copy(q).wait_send()
         part_copy(q).wait_send()
+    gd_copy.wait()
+    gu_copy.wait()
+
+
+def finish(pieces, *refs):
+    n = len(pieces)
+    given, out, held = refs[:n], refs[n:2 * n], refs[2 * n:3 * n]
+    in_sem, out_sem = refs[3 * n:]
+    steps = [(i, p) for i in range(n) for p in range(pieces[i])]
+
+    def move(i, p, source, target, sem, at):
+        span = source.shape[0] // pieces[i]
+        rows = pl.ds(p * span, span)
+        return pltpu.make_async_copy(source.at[rows], target.at[rows], sem.at[at])
+
+    for at, (i, p) in enumerate(steps):
+        move(i, p, given[i], held[i], in_sem, at).start()
+    for at, (i, p) in enumerate(steps):
+        move(i, p, given[i], held[i], in_sem, at).wait()
+        move(i, p, held[i], out[i], out_sem, at).start()
+    for at, (i, p) in enumerate(steps):
+        move(i, p, held[i], out[i], out_sem, at).wait()
 
 
 def on_device(dp_count, tensor_count, tok, w, down, up, cot, seq_index, storage):
@@ -272,7 +328,8 @@
     rows = tok.shape[0]
     seqs = seq_index.shape[0] // dp_count
     length = rows // seqs
-    groups = 2
+    groups = len(slot_groups(dp_count))
+    anywhere = pl.BlockSpec(memory_space=pl.ANY)
     wide = block + out_block
     vmem = pl.BlockSpec(memory_space=pltpu.VMEM)
     smem = pl.BlockSpec(memory_space=pltpu.SMEM)
@@ -286,17 +343,21 @@
         in_specs=[smem, smem],
         out_specs=(smem, smem),
     )(seq_index, storage)
-    return pl.pallas_call(
-        functools.partial(kernel, dp_count, tensor_count, groups),
+    results = pl.pallas_call(
+        functools.partial(kernel, dp_count, tensor_count),
         out_shape=(
             jax.ShapeDtypeStruct((rows, out_block), BF16),
             jax.ShapeDtypeStruct((rows, block), BF16),
             jax.ShapeDtypeStruct((resident, rank, block), F32),
             jax.ShapeDtypeStruct((resident, rank, out_block), F32),
         ),
-        in_specs=[smem, smem, vmem, pl.BlockSpec(memory_space=pl.ANY), vmem, vmem, vmem, vmem],
-        out_specs=(vmem, vmem, vmem, vmem),
+        in_specs=[smem, smem, vmem, anywhere, anywhere, anywhere, vmem, vmem],
+        out_specs=(vmem, vmem, anywhere, anywhere),
         scratch_shapes=[
+            pltpu.VMEM(down.shape, BF16),
+            pltpu.VMEM(up.shape, BF16),
+            pltpu.VMEM(down.shape, F32),
+            pltpu.VMEM(up.shape, F32),
             pltpu.VMEM((tensor_count, w.shape[0], out_block), BF16),
             pltpu.VMEM((dp_count * length, wide), BF16),
             pltpu.VMEM((dp_count * length, wide), BF16),
@@ -305,11 +366,12 @@
             pltpu.VMEM((tensor_count, rows, out_block), BF16),
             pltpu.VMEM((tensor_count, rows, out_block), BF16),
             pltpu.VMEM((tensor_count, rows, out_block), BF16),
-            pltpu.VMEM((groups, tensor_count, dp_count // groups * length, 2 * rank), BF16),
+            pltpu.VMEM((tensor_count, dp_count * length, 2 * rank), BF16),
             pltpu.VMEM((resident, dp_count * length, rank), BF16),
             pltpu.VMEM((resident, dp_count * length, rank), BF16),
             pltpu.VMEM((rows, block), F32),
             dma((tensor_count,)),
+            dma((4,)),
             dma((dp_count,)),
             dma((dp_count,)),
             dma((dp_count,)),
@@ -327,6 +389,15 @@
     )(
         table, weights, tok.reshape(seqs, length, block), w, down, up, cot,
         cot.reshape(seqs, length, out_block))
+    pieces = (1, 2, resident, 1)
+    return pl.pallas_call(
+        functools.partial(finish, pieces),
+        out_shape=tuple(jax.ShapeDtypeStruct(r.shape, r.dtype) for r in results),
+        in_specs=[anywhere] * 4,
+        out_specs=(anywhere,) * 4,
+        scratch_shapes=[pltpu.VMEM(r.shape, r.dtype) for r in results] + [
+            dma((sum(pieces),)), dma((sum(pieces),))],
+    )(*results)
 
 
 def solution(mesh):

time: 91 us -> 71.2 us (0.78)
  Pallas kernels: 83.2 us -> 70.3 us
  local copies, waits for them, and re-layouts: 6.95 us -> 0 us
    pallas_call x1 -> x2, Pallas kernels: 81.8 us -> 69 us  [the longest x1 66.3 us: on_device(): pl.pallas_call(functools.partial(kernel, dp_count, tensor_count), out_sha...]
    unnamed x6 -> x0, local copies, waits for them, and re-layouts: 6.95 us -> none
where the time goes in v2:
time: 71.2 us; the launch traced here: 71 us
  Pallas kernels  70.3 us (99%)
    pallas_call x1, Pallas kernels, on_device(): pl.pallas_call(functools.partial(kernel, dp_count, tensor_count), out_sha...  66.3 us
    pallas_call x1, Pallas kernels, on_device(): pl.pallas_call(functools.partial(finish, pieces), out_shape=tuple((jax.Sh...  2.66 us

profile of v2, /device:TPU:0, one launch (start us, length us, event | category | flops | bytes accessed | tf_op | source)
XLA Modules:
  0.0 71.0 jit_solution(13335015475758364166)
XLA Ops:
  0.6 1.4 %shard_map.102 = (s32[20]{0:T(128)}, f32[27]{0:T(128)}) custom-call(s32[32]{0:T(128)} %seq_ref.1, s32[24]{0:T(128)} %store_ref.1), custom_call_target="tpu_custom_call" | custom-call | tf_op jit(solution)/shard_map/pallas_call | solution.py:337
  2.0 66.3 %shard_map.103 = (bf16[128,512]{1,0:T(8,128)(2,1)}, bf16[128,2048]{1,0:T(8,128)(2,1)}, f32[3,64,2048]{2,1,0:T(8,128)}, f32[3,64,512]{2,1,0:T(8,128)}) custom-call(s32[20]{0:T(128)} %get-tuple-element.10.table_ref, f32[27]{0:T(128)} %get-tuple-element.11.weight_ref, bf16[4,32,2048]{2,1,0:T(8,128)(2,1)} %bitcast.3, bf16[2048,2048]{1,0:T(8,128)(2,1)} %w_ref.1, ...), custom_call_target="tpu_custom_call" | custom-call | tf_op jit(solution)/shard_map/pallas_call | solution.py:346
  68.3 2.7 %shard_map.104 = (bf16[128,512]{1,0:T(8,128)(2,1)}, bf16[128,2048]{1,0:T(8,128)(2,1)}, f32[3,64,2048]{2,1,0:T(8,128)}, f32[3,64,512]{2,1,0:T(8,128)}) custom-call(bf16[128,512]{1,0:T(8,128)(2,1)} %get-tuple-element.12.refs_0_, bf16[128,2048]{1,0:T(8,128)(2,1)} %get-tuple-element.13.refs_1_, f32[3,64,2048]{2,1,0:T(8,128)} %get-tuple-element.14.refs_2_, ...), custom_call_target="tpu_custom_call" | custom-call | tf_op jit(solution)/shard_map/pallas_call | solution.py:393
